TPU v7x, 256 devices: a whole 4x4x8 slice. The times are simulated.
256 devices in a mesh: dp: 16 (over y, x_lo, core), cells: 16 (over z, x_hi).
Axes of the slice: x: 4 (x_hi: 2, x_lo: 2; x = x_hi * 2 + x_lo), y: 4, z: 8, core: 2. Of those that a mesh axis runs over, the one named last changes fastest.
Arguments:
- source_field: bfloat16 [48, 8, 12288], P(None, None, 'cells'), may hold values from -85 to 85, as said below
- receiver_field: bfloat16 [512, 8, 12288], P('dp', None, 'cells'), may hold values from -6 to 6
- source_index: int32 [8192], P('dp'), may hold values from 0 to 47
- receiver_index: int32 [8192], P('dp'), may hold values from 0 to 511, as said below
- observed: float32 [8192], P('dp'), may hold values from -6 to 6
- noise_code: int32 [8, 8192], P(None, 'dp'), may hold values from -4096 to 4096
- huber_code: int32 [8], replicated, may hold values from 8 to 40
- start_model: float32 [12288], P('cells'), may hold values from -6 to 6
Outputs:
- models: float32 [8, 12288], P(None, 'cells')
Inputs may be any that keep to these rules, and one draw needn't show every extreme that they name: `source_field`: entries of order one to ten; the scale varies from cell to cell. `receiver_index`: in each aligned block of 512 data, exactly 512 // 16 data name a receiver in each range [j * 32, (j + 1) * 32).
All inputs are finite; a program needn't handle non-finite values.
Results may differ from a plain program's by a relative error of at most 0.0011.
Values may be sent and summed in bfloat16 or wider, within the bound.
A program may use at most 64 MiB of HBM per device.

v0:
```python
import math
import jax
import jax.numpy as jnp
from jax import lax
from jax.sharding import PartitionSpec as P

ITERS = 2


def on_device(
    source_field,
    receiver_field,
    source_index,
    receiver_index,
    observed,
    noise_code,
    huber_code,
    start_model,
):
    count = huber_code.shape[0]
    thresh = (huber_code.astype(jnp.float32) / 16.0)[:, None]
    shifted = observed[None, :] + noise_code.astype(jnp.float32) / 4096.0
    receivers = lax.all_gather(receiver_field, "dp", axis=0, tiled=True)
    cells_local = source_field.shape[2]
    cells_total = cells_local * lax.axis_size("cells")
    components = source_field.shape[1]
    total = jnp.zeros((source_index.shape[0], cells_local), jnp.float32)
    for component in range(components):
        factor = 1.0 if component % 2 == 0 else -1.0
        source_part = source_field[source_index, component, :].astype(jnp.float32)
        receiver_part = receivers[receiver_index, component, :].astype(jnp.float32)
        total = total + factor * (source_part * receiver_part)
    kernel = (total * (0.2 / math.sqrt(components * cells_total))).astype(jnp.bfloat16)
    models = jnp.broadcast_to(start_model[None, :], (count, cells_local))
    velocity = jnp.zeros((count, cells_local), jnp.float32)
    for iteration in range(ITERS):
        model_half = models.astype(jnp.bfloat16)
        partial_sum = lax.dot_general(
            model_half, kernel, (((1,), (1,)), ((), ())), preferred_element_type=jnp.float32
        )
        predicted = lax.psum(partial_sum, "cells")
        weighted = jnp.clip(predicted - shifted, -thresh, thresh).astype(jnp.bfloat16)
        gradient_part = jnp.dot(weighted, kernel, preferred_element_type=jnp.float32)
        gradient = lax.psum(gradient_part, "dp")
        squares = lax.psum(jnp.sum(gradient * gradient, axis=1), "cells")
        scale_now = jnp.sqrt(squares / cells_total + 1e-06)[:, None]
        velocity = 0.9 * velocity + gradient / scale_now
        models = models - 0.1 * velocity
    return models


def solution(mesh):
    placed = (
        P(None, None, "cells"),
        P("dp", None, "cells"),
        P("dp"),
        P("dp"),
        P("dp"),
        P(None, "dp"),
        P(),
        P("cells"),
    )
    return jax.shard_map(
        on_device, mesh=mesh, in_specs=placed, out_specs=P(None, "cells"), check_vma=False
    )
```

profile of v0, /device:TPU:4, one launch (start us, length us, event | category | flops | bytes accessed | tf_op | source)
XLA Modules:
  0.0 487.7 jit_solution(16038923808687295108)
XLA Ops:
  6.5 0.0 copy-start
  6.5 0.0 all-gather.2.cloned.1.call-start
  6.5 0.7 all-gather.2.cloned.1.call-update
  7.3 0.7 fusion.17
  8.0 0.0 copy-done
  8.0 4.6 gather_fusion
  12.5 4.6 gather_fusion.10
  17.1 7.2 %gather_fusion.12 = bf16[512,768]{1,0:T(8,128)(2,1)} fusion(bf16[48,8,768]{2,1,0:T(8,128)(2,1)S(1)} %copy-done, s32[512]{0:T(512)S(1)} %get-tuple-element.12), kind=kCustom, calls=%fused_computation.12 | custom fusion | bytes 1576960 | tf_op jit(solution)/shard_map/gather | solution.py:30
  24.3 7.1 %gather_fusion.14 = bf16[512,768]{1,0:T(8,128)(2,1)} fusion(bf16[48,8,768]{2,1,0:T(8,128)(2,1)S(1)} %copy-done, s32[512]{0:T(512)S(1)} %get-tuple-element.6), kind=kCustom, calls=%fused_computation.14 | custom fusion | bytes 1576960 | tf_op jit(solution)/shard_map/gather | solution.py:30
  31.4 7.1 %gather_fusion.2 = bf16[512,768]{1,0:T(8,128)(2,1)} fusion(bf16[48,8,768]{2,1,0:T(8,128)(2,1)S(1)} %copy-done, s32[512]{0:T(512)S(1)} %get-tuple-element.7), kind=kCustom, calls=%fused_computation.2 | custom fusion | bytes 1576960 | tf_op jit(solution)/shard_map/gather | solution.py:30
  38.5 7.1 %gather_fusion.4 = bf16[512,768]{1,0:T(8,128)(2,1)} fusion(bf16[48,8,768]{2,1,0:T(8,128)(2,1)S(1)} %copy-done, s32[512]{0:T(512)S(1)} %get-tuple-element.8), kind=kCustom, calls=%fused_computation.4 | custom fusion | bytes 1576960 | tf_op jit(solution)/shard_map/gather | solution.py:30
  45.6 7.2 %gather_fusion.6 = bf16[512,768]{1,0:T(8,128)(2,1)} fusion(bf16[48,8,768]{2,1,0:T(8,128)(2,1)S(1)} %copy-done, s32[512]{0:T(512)S(1)} %get-tuple-element.9), kind=kCustom, calls=%fused_computation.6 | custom fusion | bytes 1576960 | tf_op jit(solution)/shard_map/gather | solution.py:30
  52.8 0.0 copy-start.2
  52.8 0.0 copy-start.5
  52.8 0.0 copy-start.4
  52.8 7.1 %gather_fusion.8 = bf16[512,768]{1,0:T(8,128)(2,1)} fusion(bf16[48,8,768]{2,1,0:T(8,128)(2,1)S(1)} %copy-done, s32[512]{0:T(512)S(1)} %get-tuple-element.10), kind=kCustom, calls=%fused_computation.8 | custom fusion | bytes 1576960 | tf_op jit(solution)/shard_map/gather | solution.py:30
  59.9 0.0 copy-done.2
  59.9 0.0 copy-done.5
  59.9 0.0 copy-done.4
  60.0 0.0 all-gather.2.cloned.1.call-done
  60.0 9.7 %gather_fusion.1 = bf16[512,768]{1,0:T(8,128)(2,1)} fusion(bf16[512,8,768]{2,1,0:T(8,128)(2,1)} %all-gather.2.cloned.1.call-done, s32[512]{0:T(512)S(1)} %get-tuple-element.13), kind=kCustom, calls=%fused_computation.1 | custom fusion | bytes 1576960 | tf_op jit(solution)/shard_map/gather | solution.py:31
  69.7 9.7 %gather_fusion.11 = bf16[512,768]{1,0:T(8,128)(2,1)} fusion(bf16[512,8,768]{2,1,0:T(8,128)(2,1)} %all-gather.2.cloned.1.call-done, s32[512]{0:T(512)S(1)} %get-tuple-element.19), kind=kCustom, calls=%fused_computation.11 | custom fusion | bytes 1576960 | tf_op jit(solution)/shard_map/gather | solution.py:31
  79.4 9.8 %gather_fusion.13 = bf16[512,768]{1,0:T(8,128)(2,1)} fusion(bf16[512,8,768]{2,1,0:T(8,128)(2,1)} %all-gather.2.cloned.1.call-done, s32[512]{0:T(512)S(1)} %get-tuple-element.20), kind=kCustom, calls=%fused_computation.13 | custom fusion | bytes 1576960 | tf_op jit(solution)/shard_map/gather | solution.py:31
  89.2 9.7 %gather_fusion.15 = bf16[512,768]{1,0:T(8,128)(2,1)} fusion(bf16[512,8,768]{2,1,0:T(8,128)(2,1)} %all-gather.2.cloned.1.call-done, s32[512]{0:T(512)S(1)} %get-tuple-element.14), kind=kCustom, calls=%fused_computation.15 | custom fusion | bytes 1576960 | tf_op jit(solution)/shard_map/gather | solution.py:31
  98.9 9.7 %gather_fusion.3 = bf16[512,768]{1,0:T(8,128)(2,1)} fusion(bf16[512,8,768]{2,1,0:T(8,128)(2,1)} %all-gather.2.cloned.1.call-done, s32[512]{0:T(512)S(1)} %get-tuple-element.15), kind=kCustom, calls=%fused_computation.3 | custom fusion | bytes 1576960 | tf_op jit(solution)/shard_map/gather | solution.py:31
  108.6 9.7 %gather_fusion.5 = bf16[512,768]{1,0:T(8,128)(2,1)} fusion(bf16[512,8,768]{2,1,0:T(8,128)(2,1)} %all-gather.2.cloned.1.call-done, s32[512]{0:T(512)S(1)} %get-tuple-element.16), kind=kCustom, calls=%fused_computation.5 | custom fusion | bytes 1576960 | tf_op jit(solution)/shard_map/gather | solution.py:31
  118.3 9.7 %gather_fusion.7 = bf16[512,768]{1,0:T(8,128)(2,1)} fusion(bf16[512,8,768]{2,1,0:T(8,128)(2,1)} %all-gather.2.cloned.1.call-done, s32[512]{0:T(512)S(1)} %get-tuple-element.17), kind=kCustom, calls=%fused_computation.7 | custom fusion | bytes 1576960 | tf_op jit(solution)/shard_map/gather | solution.py:31
  128.0 9.7 %gather_fusion.9 = bf16[512,768]{1,0:T(8,128)(2,1)} fusion(bf16[512,8,768]{2,1,0:T(8,128)(2,1)} %all-gather.2.cloned.1.call-done, s32[512]{0:T(512)S(1)} %get-tuple-element.18), kind=kCustom, calls=%fused_computation.9 | custom fusion | bytes 1576960 | tf_op jit(solution)/shard_map/gather | solution.py:31
  137.8 0.0 copy-start.1
  137.8 0.0 copy-start.3
  137.8 6.0 %multiply_convert_fusion = bf16[512,768]{1,0:T(8,128)(2,1)S(1)} fusion(bf16[512,768]{1,0:T(8,128)(2,1)} %gather_fusion.15, bf16[512,768]{1,0:T(8,128)(2,1)} %gather_fusion.14, bf16[512,768]{1,0:T(8,128)(2,1)} %gather_fusion.13, bf16[512,768]{1,0:T(8,128)(2,1)} %gather_fusion.12, bf16[512,768]{1,0:T(8,128)(2,1)} %gather_fusion.11, ...), kind=kLoop, calls=%fused_computation.16 | loop fusion | flops 14548992 | bytes 13369344 | tf_op jit(solution)/shard_map/convert_element_type | solution.py:33
  143.8 0.3 convolution_bitcast_fusion
  144.1 74.7 %psum.42 = f32[8,512]{1,0:T(8,128)S(1)} all-reduce(f32[8,512]{1,0:T(8,128)S(1)} %convolution_bitcast_fusion), channel_id=1, replica_groups=mesh['dp'=16,'cells'=16] {'cells'}, use_global_device_ids=true, to_apply=%region_0.0 | all-reduce | flops 4096 | bytes 32768 | tf_op jit(solution)/shard_map/psum | solution.py:41
  218.8 0.0 copy-done.1
  218.8 0.0 copy-done.3
  218.8 0.2 fusion.5
  219.1 52.9 %psum.43 = f32[8,768]{1,0:T(8,128)S(1)} all-reduce(f32[8,768]{1,0:T(8,128)S(1)} %fusion.5), channel_id=1, replica_groups=mesh['dp'=16,'cells'=16] {'dp'}, use_global_device_ids=true, to_apply=%region_1.2 | all-reduce | flops 6144 | bytes 49152 | tf_op jit(solution)/shard_map/psum | solution.py:44
  272.0 0.1 multiply_reduce_fusion.1
  272.1 42.5 %psum.44 = f32[8]{0:T(128)S(1)} all-reduce(f32[8]{0:T(128)S(1)} %multiply_reduce_fusion.1), channel_id=1, replica_groups=mesh['dp'=16,'cells'=16] {'cells'}, use_global_device_ids=true, to_apply=%region_3.4 | all-reduce | flops 8 | bytes 64 | tf_op jit(solution)/shard_map/psum | solution.py:45
  314.6 0.3 fusion.1
  314.9 69.7 %psum.45 = f32[8,512]{1,0:T(8,128)S(1)} all-reduce(f32[8,512]{1,0:T(8,128)S(1)} %fusion.1), channel_id=1, replica_groups=mesh['dp'=16,'cells'=16] {'cells'}, use_global_device_ids=true, to_apply=%region_4.5 | all-reduce | flops 4096 | bytes 32768 | tf_op jit(solution)/shard_map/psum | solution.py:41
  384.6 0.2 fusion.6
  384.9 52.9 %psum.46 = f32[8,768]{1,0:T(8,128)S(1)} all-reduce(f32[8,768]{1,0:T(8,128)S(1)} %fusion.6), channel_id=1, replica_groups=mesh['dp'=16,'cells'=16] {'dp'}, use_global_device_ids=true, to_apply=%region_5.6 | all-reduce | flops 6144 | bytes 49152 | tf_op jit(solution)/shard_map/psum | solution.py:44
  437.8 0.1 multiply_reduce_fusion
  437.9 42.2 %psum.47 = f32[8]{0:T(128)S(1)} all-reduce(f32[8]{0:T(128)S(1)} %multiply_reduce_fusion), channel_id=1, replica_groups=mesh['dp'=16,'cells'=16] {'cells'}, use_global_device_ids=true, to_apply=%region_7.8 | all-reduce | flops 8 | bytes 64 | tf_op jit(solution)/shard_map/psum | solution.py:45
  480.1 0.7 multiply_subtract_fusion
  (5 shorter events, 0.0 us)
Async XLA Ops:
  6.5 1.4 copy-start
  6.5 53.4 %all-gather.2.cloned.1.call-start = ((), (), s32[]{:S(2)}) async-start(), calls=%async_computation | async-start | bytes 6684672 | tf_op jit(solution)/shard_map/all_gather | solution.py:23
  52.8 7.1 %copy-start.2 = (f32[768]{0:T(1024)S(1)}, f32[768]{0:T(1024)}, u32[]{:S(2)}) copy-start(f32[768]{0:T(1024)} %param.15) | copy-start | bytes 9220
  52.8 7.1 %copy-start.5 = (s32[8]{0:T(128)S(1)}, s32[8]{0:T(128)}, u32[]{:S(2)}) copy-start(s32[8]{0:T(128)} %param.14) | copy-start | bytes 100
  52.8 7.2 %copy-start.4 = (s32[512]{0:T(512)S(1)}, s32[512]{0:T(512)}, u32[]{:S(2)}) copy-start(s32[512]{0:T(512)} %param.11) | copy-start | bytes 6148
  137.8 81.0 %copy-start.1 = (s32[8,512]{1,0:T(8,128)S(1)}, s32[8,512]{1,0:T(8,128)}, u32[]{:S(2)}) copy-start(s32[8,512]{1,0:T(8,128)} %param.13) | copy-start | bytes 49156
  137.8 81.0 %copy-start.3 = (f32[512]{0:T(512)S(1)}, f32[512]{0:T(512)}, u32[]{:S(2)}) copy-start(f32[512]{0:T(512)} %param.12) | copy-start | bytes 6148
Sparse Core Ops, SparseCore 0:
  9.2 47.6 all-gather.1
where the time goes:
time: 489 us; the launch traced here: 488 us
  blocking collectives  335 us (69%)
  local copies, waits for them, and re-layouts  130 us (27%)
  between operations  13.5 us (3%)
  other arithmetic  7.68 us (2%)
    psum x2, blocking collectives, on_device(): predicted = lax.psum(partial_sum, 'cells')  144 us
    psum x2, blocking collectives, on_device(): gradient = lax.psum(gradient_part, 'dp')  106 us
    psum x2, blocking collectives, on_device(): squares = lax.psum(jnp.sum(gradient * gradient, axis=1), 'cells')  84.7 us
    gather x8, local copies, waits for them, and re-layouts, on_device(): receiver_part = receivers[receiver_index, component, :].astype(jnp.float32)  77.8 us
    gather x8, local copies, waits for them, and re-layouts, on_device(): source_part = source_field[source_index, component, :].astype(jnp.float32)  51.9 us
  transfers between devices with their start and end apart: 1, of which 0 were waited for; matrix products, arithmetic and copies ran while one was open for 11% of the time, Pallas kernels for 0%

commit v1 on v0

--- a/solution.py
+++ b/solution.py
@@ -38,7 +38,7 @@
         partial_sum = lax.dot_general(
             model_half, kernel, (((1,), (1,)), ((), ())), preferred_element_type=jnp.float32
         )
-        predicted = lax.psum(partial_sum, "cells")
+        predicted = jnp.sum(lax.all_gather(partial_sum, "cells"), axis=0)
         weighted = jnp.clip(predicted - shifted, -thresh, thresh).astype(jnp.bfloat16)
         gradient_part = jnp.dot(weighted, kernel, preferred_element_type=jnp.float32)
         gradient = lax.psum(gradient_part, "dp")

time: 489 us -> 419 us (0.86)
  blocking collectives: 335 us -> 265 us
    psum x2 -> x0, blocking collectives: 144 us -> none  [on_device(): predicted = lax.psum(partial_sum, 'cells')]
    all_gather x0 -> x2, blocking collectives: none -> 77.6 us  [on_device(): predicted = jnp.sum(lax.all_gather(partial_sum, 'cells'), axis=0)]
  transfers between devices with their start and end apart: 1 -> 1, of which waited for: 0 -> 0; matrix products, arithmetic and copies ran while one was open for 11% -> 13% of each run, Pallas kernels for 0% -> 0%
where the time goes in v1:
time: 419 us; the launch traced here: 418 us
  blocking collectives  265 us (63%)
  local copies, waits for them, and re-layouts  130 us (31%)
  between operations  13.5 us (3%)
  other arithmetic  7.72 us (2%)
    psum x2, blocking collectives, on_device(): gradient = lax.psum(gradient_part, 'dp')  107 us
    psum x2, blocking collectives, on_device(): squares = lax.psum(jnp.sum(gradient * gradient, axis=1), 'cells')  80.9 us
    gather x8, local copies, waits for them, and re-layouts, on_device(): receiver_part = receivers[receiver_index, component, :].astype(jnp.float32)  77.8 us
    all_gather x2, blocking collectives, on_device(): predicted = jnp.sum(lax.all_gather(partial_sum, 'cells'), axis=0)  77.6 us
    gather x8, local copies, waits for them, and re-layouts, on_device(): source_part = source_field[source_index, component, :].astype(jnp.float32)  51.9 us
  transfers between devices with their start and end apart: 1, of which 0 were waited for; matrix products, arithmetic and copies ran while one was open for 13% of the time, Pallas kernels for 0%

profile of v1, /device:TPU:4, one launch (start us, length us, event | category | flops | bytes accessed | tf_op | source)
XLA Modules:
  0.0 418.0 jit_solution(6154154334488081067)
XLA Ops:
  6.5 0.0 copy-start
  6.5 0.0 all-gather.4.cloned.1.call-start
  6.5 0.7 all-gather.4.cloned.1.call-update
  7.3 0.7 fusion.17
  8.0 0.0 copy-done
  8.0 4.6 %gather_fusion = bf16[512,768]{1,0:T(8,128)(2,1)S(1)} fusion(bf16[48,8,768]{2,1,0:T(8,128)(2,1)S(1)} %copy-done, s32[512]{0:T(512)S(1)} %get-tuple-element.5), kind=kCustom, calls=%fused_computation | custom fusion | bytes 1576960 | tf_op jit(solution)/shard_map/gather | solution.py:30
  12.5 4.6 %gather_fusion.10 = bf16[512,768]{1,0:T(8,128)(2,1)S(1)} fusion(bf16[48,8,768]{2,1,0:T(8,128)(2,1)S(1)} %copy-done, s32[512]{0:T(512)S(1)} %get-tuple-element.11), kind=kCustom, calls=%fused_computation.10 | custom fusion | bytes 1576960 | tf_op jit(solution)/shard_map/gather | solution.py:30
  17.1 7.2 %gather_fusion.12 = bf16[512,768]{1,0:T(8,128)(2,1)} fusion(bf16[48,8,768]{2,1,0:T(8,128)(2,1)S(1)} %copy-done, s32[512]{0:T(512)S(1)} %get-tuple-element.12), kind=kCustom, calls=%fused_computation.12 | custom fusion | bytes 1576960 | tf_op jit(solution)/shard_map/gather | solution.py:30
  24.3 7.1 %gather_fusion.14 = bf16[512,768]{1,0:T(8,128)(2,1)} fusion(bf16[48,8,768]{2,1,0:T(8,128)(2,1)S(1)} %copy-done, s32[512]{0:T(512)S(1)} %get-tuple-element.6), kind=kCustom, calls=%fused_computation.14 | custom fusion | bytes 1576960 | tf_op jit(solution)/shard_map/gather | solution.py:30
  31.4 7.1 %gather_fusion.2 = bf16[512,768]{1,0:T(8,128)(2,1)} fusion(bf16[48,8,768]{2,1,0:T(8,128)(2,1)S(1)} %copy-done, s32[512]{0:T(512)S(1)} %get-tuple-element.7), kind=kCustom, calls=%fused_computation.2 | custom fusion | bytes 1576960 | tf_op jit(solution)/shard_map/gather | solution.py:30
  38.5 7.1 %gather_fusion.4 = bf16[512,768]{1,0:T(8,128)(2,1)} fusion(bf16[48,8,768]{2,1,0:T(8,128)(2,1)S(1)} %copy-done, s32[512]{0:T(512)S(1)} %get-tuple-element.8), kind=kCustom, calls=%fused_computation.4 | custom fusion | bytes 1576960 | tf_op jit(solution)/shard_map/gather | solution.py:30
  45.6 7.2 %gather_fusion.6 = bf16[512,768]{1,0:T(8,128)(2,1)} fusion(bf16[48,8,768]{2,1,0:T(8,128)(2,1)S(1)} %copy-done, s32[512]{0:T(512)S(1)} %get-tuple-element.9), kind=kCustom, calls=%fused_computation.6 | custom fusion | bytes 1576960 | tf_op jit(solution)/shard_map/gather | solution.py:30
  52.8 0.0 copy-start.2
  52.8 0.0 copy-start.5
  52.8 0.0 copy-start.4
  52.8 7.1 %gather_fusion.8 = bf16[512,768]{1,0:T(8,128)(2,1)} fusion(bf16[48,8,768]{2,1,0:T(8,128)(2,1)S(1)} %copy-done, s32[512]{0:T(512)S(1)} %get-tuple-element.10), kind=kCustom, calls=%fused_computation.8 | custom fusion | bytes 1576960 | tf_op jit(solution)/shard_map/gather | solution.py:30
  59.9 0.0 copy-done.2
  59.9 0.0 copy-done.5
  59.9 0.0 copy-done.4
  60.0 0.0 all-gather.4.cloned.1.call-done
  60.0 9.7 %gather_fusion.1 = bf16[512,768]{1,0:T(8,128)(2,1)} fusion(bf16[512,8,768]{2,1,0:T(8,128)(2,1)} %all-gather.4.cloned.1.call-done, s32[512]{0:T(512)S(1)} %get-tuple-element.13), kind=kCustom, calls=%fused_computation.1 | custom fusion | bytes 1576960 | tf_op jit(solution)/shard_map/gather | solution.py:31
  69.7 9.7 %gather_fusion.11 = bf16[512,768]{1,0:T(8,128)(2,1)} fusion(bf16[512,8,768]{2,1,0:T(8,128)(2,1)} %all-gather.4.cloned.1.call-done, s32[512]{0:T(512)S(1)} %get-tuple-element.19), kind=kCustom, calls=%fused_computation.11 | custom fusion | bytes 1576960 | tf_op jit(solution)/shard_map/gather | solution.py:31
  79.4 9.8 %gather_fusion.13 = bf16[512,768]{1,0:T(8,128)(2,1)} fusion(bf16[512,8,768]{2,1,0:T(8,128)(2,1)} %all-gather.4.cloned.1.call-done, s32[512]{0:T(512)S(1)} %get-tuple-element.20), kind=kCustom, calls=%fused_computation.13 | custom fusion | bytes 1576960 | tf_op jit(solution)/shard_map/gather | solution.py:31
  89.2 9.7 %gather_fusion.15 = bf16[512,768]{1,0:T(8,128)(2,1)} fusion(bf16[512,8,768]{2,1,0:T(8,128)(2,1)} %all-gather.4.cloned.1.call-done, s32[512]{0:T(512)S(1)} %get-tuple-element.14), kind=kCustom, calls=%fused_computation.15 | custom fusion | bytes 1576960 | tf_op jit(solution)/shard_map/gather | solution.py:31
  98.9 9.7 %gather_fusion.3 = bf16[512,768]{1,0:T(8,128)(2,1)} fusion(bf16[512,8,768]{2,1,0:T(8,128)(2,1)} %all-gather.4.cloned.1.call-done, s32[512]{0:T(512)S(1)} %get-tuple-element.15), kind=kCustom, calls=%fused_computation.3 | custom fusion | bytes 1576960 | tf_op jit(solution)/shard_map/gather | solution.py:31
  108.6 9.7 %gather_fusion.5 = bf16[512,768]{1,0:T(8,128)(2,1)} fusion(bf16[512,8,768]{2,1,0:T(8,128)(2,1)} %all-gather.4.cloned.1.call-done, s32[512]{0:T(512)S(1)} %get-tuple-element.16), kind=kCustom, calls=%fused_computation.5 | custom fusion | bytes 1576960 | tf_op jit(solution)/shard_map/gather | solution.py:31
  118.3 9.7 %gather_fusion.7 = bf16[512,768]{1,0:T(8,128)(2,1)} fusion(bf16[512,8,768]{2,1,0:T(8,128)(2,1)} %all-gather.4.cloned.1.call-done, s32[512]{0:T(512)S(1)} %get-tuple-element.17), kind=kCustom, calls=%fused_computation.7 | custom fusion | bytes 1576960 | tf_op jit(solution)/shard_map/gather | solution.py:31
  128.0 9.7 %gather_fusion.9 = bf16[512,768]{1,0:T(8,128)(2,1)} fusion(bf16[512,8,768]{2,1,0:T(8,128)(2,1)} %all-gather.4.cloned.1.call-done, s32[512]{0:T(512)S(1)} %get-tuple-element.18), kind=kCustom, calls=%fused_computation.9 | custom fusion | bytes 1576960 | tf_op jit(solution)/shard_map/gather | solution.py:31
  137.8 0.0 copy-start.1
  137.8 0.0 copy-start.3
  137.8 6.0 %multiply_convert_fusion = bf16[512,768]{1,0:T(8,128)(2,1)S(1)} fusion(bf16[512,768]{1,0:T(8,128)(2,1)} %gather_fusion.15, bf16[512,768]{1,0:T(8,128)(2,1)} %gather_fusion.14, bf16[512,768]{1,0:T(8,128)(2,1)} %gather_fusion.13, bf16[512,768]{1,0:T(8,128)(2,1)} %gather_fusion.12, bf16[512,768]{1,0:T(8,128)(2,1)} %gather_fusion.11, ...), kind=kLoop, calls=%fused_computation.16 | loop fusion | flops 14548992 | bytes 13369344 | tf_op jit(solution)/shard_map/convert_element_type | solution.py:33
  143.8 0.3 convolution_bitcast_fusion
  144.1 40.6 %all-gather = f32[128,512]{1,0:T(8,128)S(1)} all-gather(f32[8,512]{1,0:T(8,128)S(1)} %convolution_bitcast_fusion), channel_id=2, replica_groups=mesh['dp'=16,'cells'=16] {'cells'}, dimensions={0}, use_global_device_ids=true | all-gather | bytes 278528 | tf_op jit(solution)/shard_map/all_gather | solution.py:41
  184.7 0.0 copy-done.1
  184.7 0.0 copy-done.3
  184.7 0.2 fusion.5
  185.0 53.8 %psum.28 = f32[8,768]{1,0:T(8,128)S(1)} all-reduce(f32[8,768]{1,0:T(8,128)S(1)} %fusion.5), channel_id=1, replica_groups=mesh['dp'=16,'cells'=16] {'dp'}, use_global_device_ids=true, to_apply=%region_1.2 | all-reduce | flops 6144 | bytes 49152 | tf_op jit(solution)/shard_map/psum | solution.py:44
  238.8 0.1 multiply_reduce_fusion.1
  238.9 40.9 %psum.29 = f32[8]{0:T(128)S(1)} all-reduce(f32[8]{0:T(128)S(1)} %multiply_reduce_fusion.1), channel_id=1, replica_groups=mesh['dp'=16,'cells'=16] {'cells'}, use_global_device_ids=true, to_apply=%region_3.4 | all-reduce | flops 8 | bytes 64 | tf_op jit(solution)/shard_map/psum | solution.py:45
  279.8 0.3 fusion.1
  280.1 37.0 %all-gather.1 = f32[128,512]{1,0:T(8,128)S(1)} all-gather(f32[8,512]{1,0:T(8,128)S(1)} %fusion.1), channel_id=3, replica_groups=mesh['dp'=16,'cells'=16] {'cells'}, dimensions={0}, use_global_device_ids=true | all-gather | bytes 278528 | tf_op jit(solution)/shard_map/all_gather | solution.py:41
  317.2 0.2 fusion.6
  317.4 52.9 %psum.30 = f32[8,768]{1,0:T(8,128)S(1)} all-reduce(f32[8,768]{1,0:T(8,128)S(1)} %fusion.6), channel_id=1, replica_groups=mesh['dp'=16,'cells'=16] {'dp'}, use_global_device_ids=true, to_apply=%region_5.6 | all-reduce | flops 6144 | bytes 49152 | tf_op jit(solution)/shard_map/psum | solution.py:44
  370.3 0.1 multiply_reduce_fusion
  370.4 40.0 %psum.31 = f32[8]{0:T(128)S(1)} all-reduce(f32[8]{0:T(128)S(1)} %multiply_reduce_fusion), channel_id=1, replica_groups=mesh['dp'=16,'cells'=16] {'cells'}, use_global_device_ids=true, to_apply=%region_7.8 | all-reduce | flops 8 | bytes 64 | tf_op jit(solution)/shard_map/psum | solution.py:45
  410.5 0.7 multiply_subtract_fusion
  (7 shorter events, 0.1 us)
Async XLA Ops:
  6.5 1.4 copy-start
  6.5 53.4 %all-gather.4.cloned.1.call-start = ((), (), s32[]{:S(2)}) async-start(), calls=%async_computation | async-start | bytes 6684672 | tf_op jit(solution)/shard_map/all_gather | solution.py:23
  52.8 7.1 %copy-start.2 = (f32[768]{0:T(1024)S(1)}, f32[768]{0:T(1024)}, u32[]{:S(2)}) copy-start(f32[768]{0:T(1024)} %param.15) | copy-start | bytes 9220
  52.8 7.1 %copy-start.5 = (s32[8]{0:T(128)S(1)}, s32[8]{0:T(128)}, u32[]{:S(2)}) copy-start(s32[8]{0:T(128)} %param.14) | copy-start | bytes 100
  52.8 7.2 %copy-start.4 = (s32[512]{0:T(512)S(1)}, s32[512]{0:T(512)}, u32[]{:S(2)}) copy-start(s32[512]{0:T(512)} %param.11) | copy-start | bytes 6148
  137.8 46.9 %copy-start.1 = (s32[8,512]{1,0:T(8,128)S(1)}, s32[8,512]{1,0:T(8,128)}, u32[]{:S(2)}) copy-start(s32[8,512]{1,0:T(8,128)} %param.13) | copy-start | bytes 49156
  137.8 47.0 %copy-start.3 = (f32[512]{0:T(512)S(1)}, f32[512]{0:T(512)}, u32[]{:S(2)}) copy-start(f32[512]{0:T(512)} %param.12) | copy-start | bytes 6148
Sparse Core Ops, SparseCore 0:
  9.2 47.6 all-gather.3
